TPU v7x, 256 devices: a whole 4x4x8 slice. The times are simulated.
256 devices in a mesh: branch: 2 (over y_lo), seq: 16 (over z, core), mp: 8 (over x, y_hi).
Axes of the slice: x: 4, y: 4 (y_hi: 2, y_lo: 2; y = y_hi * 2 + y_lo), z: 8, core: 2. Of those that a mesh axis runs over, the one named last changes fastest.
Arguments:
- queries: bfloat16 [2, 16, 2048, 2048], P('branch', 'mp', 'seq'), may hold values from -8 to 8
- keys: bfloat16 [2, 16, 2048, 2048], P('branch', 'mp', 'seq'), may hold values from -8 to 8
- values: bfloat16 [2, 16, 2048, 2048], P('branch', 'mp', 'seq'), may hold values from -6 to 6
- inject: float32 [2, 16], P('branch'), may hold values from 0.2 to 0.8
- keyframes: int32 [2], replicated, may hold values from 0 to 15, as said below
- key_mask: int32 [16, 2], replicated, may hold values 0 or 1
Outputs:
- attended: bfloat16 [2, 16, 2048, 2048], P('branch', 'mp', 'seq')
Inputs may be any that keep to these rules, and one draw needn't show every extreme that they name: The keyframes are distinct frames; one of them is the last frame.
All inputs are finite; a program needn't handle non-finite values.
Results may differ from a plain program's by a relative error of at most 0.0061.
Values may be sent and summed in bfloat16 or wider, within the bound.
No kernel may reach another device: no remote copies, remote signals or barrier semaphores. Data moves between devices by JAX's collectives and lax.ppermute only.
A program may use at most 64 MiB of HBM per device.

v0:
```python
import math
import jax
import jax.numpy as jnp
from jax import lax
from jax.sharding import PartitionSpec as P

HEAD = 128
NEG_FILL = -1e30


def swapped(value, axis, bit):
    mask = 2**bit
    pairs = [(source, source ^ mask) for source in range(lax.axis_size(axis))]
    return lax.ppermute(value, axis, pairs)


def from_root(block, axis, holder):
    block = jnp.where(lax.axis_index(axis) == holder, block, jnp.zeros_like(block))
    return lax.psum(block, axis)


def blend_pair(source, partner, strength):
    return (
        (1.0 - strength) * source.astype(jnp.float32) + strength * partner.astype(jnp.float32)
    ).astype(jnp.bfloat16)


def score_tile(query_block, key_tile):
    return jnp.einsum("qhd,khd->hqk", query_block, key_tile, preferred_element_type=jnp.float32) * (
        1.0 / math.sqrt(HEAD)
    )


def attend_frame(query_rows, key_own, value_own, key_extra, value_extra, mask_row):
    frame_rows = query_rows.shape[0]
    row_width = query_rows.shape[1]
    local_heads = row_width // HEAD
    rows_block = min(512, frame_rows)
    key_count = key_extra.shape[0]
    split_queries = query_rows.reshape(frame_rows // rows_block, rows_block, local_heads, HEAD)
    key_own = key_own.reshape(frame_rows, local_heads, HEAD)
    value_own = value_own.reshape(frame_rows, local_heads, HEAD)
    key_extra = key_extra.reshape(key_count, frame_rows, local_heads, HEAD)
    value_extra = value_extra.reshape(key_count, frame_rows, local_heads, HEAD)
    present = mask_row > 0
    valid_keys = jnp.concatenate(
        [jnp.ones((frame_rows,), jnp.bool_), jnp.repeat(present, frame_rows)]
    )
    key_whole = jnp.concatenate(
        [key_own, key_extra.reshape(key_count * frame_rows, local_heads, HEAD)], axis=0
    )
    value_whole = jnp.concatenate(
        [value_own, value_extra.reshape(key_count * frame_rows, local_heads, HEAD)], axis=0
    )

    def one_block(query_block):
        scores = score_tile(query_block, key_whole)
        scores = jnp.where(valid_keys[None, None, :], scores, NEG_FILL)
        row_max = jnp.max(scores, axis=2, keepdims=True)
        weights = jnp.where(valid_keys[None, None, :], jnp.exp(scores - row_max), 0.0)
        totals = jnp.sum(weights, axis=2)
        rounded = weights.astype(jnp.bfloat16)
        mixed_out = jnp.einsum(
            "hqk,khd->qhd", rounded, value_whole, preferred_element_type=jnp.float32
        )
        result = mixed_out / jnp.transpose(totals)[:, :, None]
        return result.reshape(rows_block, row_width).astype(jnp.bfloat16)

    return lax.map(one_block, split_queries).reshape(frame_rows, row_width)


def local(queries, keys, values, inject, keyframes, key_mask):
    frames_dev = queries.shape[1]
    total_heads = inject.shape[1]
    strength = jnp.repeat(inject[0], HEAD, total_repeat_length=total_heads * HEAD)
    partner_queries, partner_keys = swapped((queries, keys), "branch", 0)
    mixed_queries = blend_pair(queries, partner_queries, strength)
    mixed_keys = blend_pair(keys, partner_keys, strength)
    head_queries, head_keys, head_values = (
        lax.all_to_all(mixed_queries, "seq", split_axis=3, concat_axis=2, tiled=True),
        lax.all_to_all(mixed_keys, "seq", split_axis=3, concat_axis=2, tiled=True),
        lax.all_to_all(values, "seq", split_axis=3, concat_axis=2, tiled=True),
    )
    frame_keys = head_keys[0]
    frame_values = head_values[0]
    mp_index = lax.axis_index("mp")
    extra_keys = []
    extra_values = []
    for keyframe_slot in range(keyframes.shape[0]):
        chosen = keyframes[keyframe_slot]
        local_slot = chosen % frames_dev
        chosen_key = lax.dynamic_index_in_dim(frame_keys, local_slot, 0, keepdims=False)
        chosen_value = lax.dynamic_index_in_dim(frame_values, local_slot, 0, keepdims=False)
        got_key, got_value = (
            from_root(chosen_key, "mp", chosen // frames_dev),
            from_root(chosen_value, "mp", chosen // frames_dev),
        )
        extra_keys.append(got_key)
        extra_values.append(got_value)
    key_extra = jnp.stack(extra_keys)
    value_extra = jnp.stack(extra_values)
    outputs = []
    for local_frame in range(frames_dev):
        mask_row = lax.dynamic_index_in_dim(
            key_mask, mp_index * frames_dev + local_frame, 0, keepdims=False
        )
        outputs.append(
            attend_frame(
                head_queries[0, local_frame],
                frame_keys[local_frame],
                frame_values[local_frame],
                key_extra,
                value_extra,
                mask_row,
            )
        )
    attended = jnp.stack(outputs)[None]
    return lax.all_to_all(attended, "seq", split_axis=2, concat_axis=3, tiled=True)


def solution(mesh):
    return jax.shard_map(
        local,
        mesh=mesh,
        in_specs=(
            P("branch", "mp", "seq", None),
            P("branch", "mp", "seq", None),
            P("branch", "mp", "seq", None),
            P("branch", None),
            P(),
            P(),
        ),
        out_specs=P("branch", "mp", "seq", None),
        check_vma=False,
    )
```

profile of v0, /device:TPU:1, one launch (start us, length us, event | category | flops | bytes accessed | tf_op | source)
XLA Modules:
  0.0 387.3 jit_solution(7415376909329658251)
XLA Ops:
  6.5 3.7 copy.89
  10.2 10.0 %all-to-all-start.2 = ((bf16[1,2,128,2048]{2,1,0,3:T(2,128)(2,1)}), bf16[1,2,128,2048]{2,1,0,3:T(2,128)(2,1)S(1)}, u32[]{:S(2)}, u32[]{:S(2)}) async-start(bf16[1,2,128,2048]{2,1,0,3:T(2,128)(2,1)} %copy.89), calls=%async_computation.2 | async-start | bytes 2097152 | tf_op jit(solution)/shard_map/all_to_all | solution.py:82
  20.2 1.3 collective-permute-start
  21.6 1.9 fusion.86
  23.6 4.3 %compare_select_fusion.1 = (f32[2048,1]{0,1:T(1,128)S(1)}, s32[2048,1]{0,1:T(1,128)S(1)}) fusion(f32[]{:T(128)} %bitcast.27, f32[]{:T(128)} %bitcast.28, f32[]{:T(128)} %bitcast.29, f32[]{:T(128)} %bitcast.30, f32[]{:T(128)} %bitcast.31, f32[]{:T(128)} %bitcast.33, f32[]{:T(128)} %bitcast.32, s32[2048,1]{0,1:T(1,128)S(1)} %bitcast.185, ...), kind=kLoop, calls=%fused_computation.65 | loop fusion | flops 28672 | bytes 32796 | tf_op jit(solution)/shard_map/jit(_take)/gather | solution.py:75
  28.1 5.7 %broadcast_subtract_fusion = (f32[2048]{0:T(1024)S(1)}, f32[2048]{0:T(1024)S(1)}) fusion(pred[2048]{0:T(1024)(128)(4,1)S(1)} %get-tuple-element.163, pred[2048]{0:T(1024)(128)(4,1)S(1)} %get-tuple-element.162, pred[2048]{0:T(1024)(128)(4,1)S(1)} %get-tuple-element.161, pred[2048]{0:T(1024)(128)(4,1)S(1)} %get-tuple-element.160, ...), kind=kLoop, calls=%fused_computation.76 | loop fusion | flops 38912 | bytes 43044 | tf_op jit(solution)/shard_map/sub | solution.py:24
  33.8 11.1 %collective-permute-done = bf16[1,2,128,2048]{3,2,1,0:T(8,128)(2,1)S(1)} collective-permute-done((bf16[1,2,128,2048]{3,2,1,0:T(8,128)(2,1)}, bf16[1,2,128,2048]{3,2,1,0:T(8,128)(2,1)S(1)}, u32[]{:S(2)}, u32[]{:S(2)}) %collective-permute-start) | collective-permute-done | bytes 1048608 | tf_op jit(solution)/shard_map/ppermute | solution.py:14
  44.9 22.5 %collective-permute-done.1 = bf16[1,2,128,2048]{3,2,1,0:T(8,128)(2,1)S(1)} collective-permute-done((bf16[1,2,128,2048]{3,2,1,0:T(8,128)(2,1)}, bf16[1,2,128,2048]{3,2,1,0:T(8,128)(2,1)S(1)}, u32[]{:S(2)}, u32[]{:S(2)}) %collective-permute-start.1) | collective-permute-done | bytes 1048608 | tf_op jit(solution)/shard_map/ppermute | solution.py:14
  67.4 2.4 add_convert_fusion
  69.8 2.0 copy.85
  71.8 7.9 %all-to-all-start.1 = ((bf16[1,2,128,2048]{2,1,0,3:T(2,128)(2,1)}), bf16[1,2,128,2048]{2,1,0,3:T(2,128)(2,1)S(1)}, u32[]{:S(2)}, u32[]{:S(2)}) async-start(bf16[1,2,128,2048]{2,1,0,3:T(2,128)(2,1)} %copy.85), calls=%async_computation.1 | async-start | bytes 2097152 | tf_op jit(solution)/shard_map/all_to_all | solution.py:81
  79.7 2.0 copy.83
  81.7 26.0 %all-to-all-done.1 = bf16[1,2,128,2048]{2,1,0,3:T(2,128)(2,1)S(1)} async-done(((bf16[1,2,128,2048]{2,1,0,3:T(2,128)(2,1)}), bf16[1,2,128,2048]{2,1,0,3:T(2,128)(2,1)S(1)}, u32[]{:S(2)}, u32[]{:S(2)}) %all-to-all-start.1) | async-done | bytes 1048608 | tf_op jit(solution)/shard_map/all_to_all | solution.py:81
  107.7 1.0 copy-done
  108.7 3.6 all-to-all-start
  118.3 1.3 copy.92
  119.7 1.4 copy.86
  121.0 1.3 copy.88
  122.4 2.9 dynamic-slice_select_fusion.1
  125.8 1.1 fusion.82
  126.8 1.3 copy.91
  128.2 1.3 copy.95
  129.5 1.1 fusion.83
  130.5 2.1 copy.87
  132.6 2.1 copy.94
  134.7 5.5 %all-to-all-done = bf16[1,2,128,2048]{2,1,0,3:T(2,128)(2,1)S(1)} async-done(((bf16[1,2,128,2048]{2,1,0,3:T(2,128)(2,1)}), bf16[1,2,128,2048]{2,1,0,3:T(2,128)(2,1)S(1)}, u32[]{:S(2)}, u32[]{:S(2)}) %all-to-all-start) | async-done | bytes 1048608 | tf_op jit(solution)/shard_map/all_to_all | solution.py:80
  140.1 0.9 copy.84
  141.1 1.0 fusion.84
  142.1 97.8 %all-reduce.5.cloned.1.call-done = (bf16[1,2048,128]{2,1,0:T(8,128)(2,1)}, bf16[1,2048,128]{2,1,0:T(8,128)(2,1)}, bf16[1,2048,128]{2,1,0:T(8,128)(2,1)}, bf16[1,2048,128]{2,1,0:T(8,128)(2,1)}) async-done(((bf16[1,2048,128]{2,1,0:T(8,128)(2,1)}, bf16[1,2048,128]{2,1,0:T(8,128)(2,1)}, bf16[1,2048,128]{2,1,0:T(8,128)(2,1)}, bf16[1,2048,128]{2,1,0:T(8,128)(2,1)}), (bf16[1,2048,128]{2,1,0:T(8,128)(2,1)}, ...) | async-done | bytes 2097168 | tf_op jit(solution)/shard_map/psum | solution.py:19
  239.9 1.4 pad_maximum_fusion.5
  241.3 1.3 pad_maximum_fusion.4
  242.6 1.9 pad_maximum_fusion.3
  244.7 0.9 broadcast.203.clone.1
  245.6 42.6 %while.21 = (s32[]{:T(128)}, bf16[4,512,128]{2,1,0:T(8,128)(2,1)}, pred[6144]{0:T(1024)(128)(4,1)S(1)}, bf16[4,512,1,128]{3,1,2,0:T(8,128)(2,1)}, bf16[6144,1,12...) while((s32[]{:T(128)}, bf16[4,512,128]{2,1,0:T(8,128)(2,1)}, ...), condition=%wide.region_7.8_spmd, body=%wide.region_4.7_spmd.sunk | while | flops 1651637248 | bytes 47477864 | solution.py:69
  245.6 3.0 fusion.99
  248.6 3.3 fusion.100
  251.9 4.3 %fusion.101 = bf16[4,512,128]{2,1,0:T(8,128)(2,1)} fusion(bf16[4,512,128]{2,1,0:T(8,128)(2,1)} %get-tuple-element.349, s32[]{:T(128)} %get-tuple-element.348, bf16[6144,1,128]{2,0,1:T(8,128)(2,1)S(1)} %copy-done.4, f32[512,6144]{1,0:T(8,128)S(1)} %get-tuple-element.310, f32[512]{0:T(512)S(1)} %get-tuple-element.311, ...), kind=kOutput, calls=%fused_computation.14.clone.1 | convolution fusion | flops 821166080 | bytes 14297600 | tf_op jit(solution)/shard_map/while/body/eval_jaxpr/hqk,khd->qhd/dot_general | solution.py:63
  256.2 3.0 fusion.99
  259.3 3.3 fusion.100
  262.6 4.3 %fusion.101 = bf16[4,512,128]{2,1,0:T(8,128)(2,1)} fusion(bf16[4,512,128]{2,1,0:T(8,128)(2,1)} %get-tuple-element.349, s32[]{:T(128)} %get-tuple-element.348, bf16[6144,1,128]{2,0,1:T(8,128)(2,1)S(1)} %copy-done.4, f32[512,6144]{1,0:T(8,128)S(1)} %get-tuple-element.310, f32[512]{0:T(512)S(1)} %get-tuple-element.311, ...), kind=kOutput, calls=%fused_computation.14.clone.1 | convolution fusion | flops 821166080 | bytes 14297600 | tf_op jit(solution)/shard_map/while/body/eval_jaxpr/hqk,khd->qhd/dot_general | solution.py:63
  266.9 3.0 fusion.99
  269.9 3.3 fusion.100
  273.2 4.3 %fusion.101 = bf16[4,512,128]{2,1,0:T(8,128)(2,1)} fusion(bf16[4,512,128]{2,1,0:T(8,128)(2,1)} %get-tuple-element.349, s32[]{:T(128)} %get-tuple-element.348, bf16[6144,1,128]{2,0,1:T(8,128)(2,1)S(1)} %copy-done.4, f32[512,6144]{1,0:T(8,128)S(1)} %get-tuple-element.310, f32[512]{0:T(512)S(1)} %get-tuple-element.311, ...), kind=kOutput, calls=%fused_computation.14.clone.1 | convolution fusion | flops 821166080 | bytes 14297600 | tf_op jit(solution)/shard_map/while/body/eval_jaxpr/hqk,khd->qhd/dot_general | solution.py:63
  277.5 3.0 fusion.99
  280.6 3.3 fusion.100
  283.9 4.3 %fusion.101 = bf16[4,512,128]{2,1,0:T(8,128)(2,1)} fusion(bf16[4,512,128]{2,1,0:T(8,128)(2,1)} %get-tuple-element.349, s32[]{:T(128)} %get-tuple-element.348, bf16[6144,1,128]{2,0,1:T(8,128)(2,1)S(1)} %copy-done.4, f32[512,6144]{1,0:T(8,128)S(1)} %get-tuple-element.310, f32[512]{0:T(512)S(1)} %get-tuple-element.311, ...), kind=kOutput, calls=%fused_computation.14.clone.1 | convolution fusion | flops 821166080 | bytes 14297600 | tf_op jit(solution)/shard_map/while/body/eval_jaxpr/hqk,khd->qhd/dot_general | solution.py:63
  288.3 40.7 %while.22 = (s32[]{:T(128)}, bf16[4,512,128]{2,1,0:T(8,128)(2,1)S(1)}, pred[6144]{0:T(1024)(128)(4,1)S(1)}, bf16[4,512,1,128]{3,1,2,0:T(8,128)(2,1)}, bf16[6144,...) while((s32[]{:T(128)}, bf16[4,512,128]{2,1,0:T(8,128)(2,1)S(1)}, ...), condition=%wide.region_11.12_spmd, body=%wide.region_8.11_spmd.sunk | while | flops 1651637248 | bytes 47477356 | solution.py:69
  288.5 3.0 fusion.104
  291.5 3.3 fusion.105
  294.8 3.8 fusion.106
  298.6 3.0 fusion.104
  301.6 3.3 fusion.105
  304.9 3.8 fusion.106
  308.7 3.0 fusion.104
  311.7 3.3 fusion.105
  315.0 3.8 fusion.106
  318.8 3.0 fusion.104
  321.9 3.3 fusion.105
  325.1 3.8 fusion.106
  328.9 1.1 maximum_bitcast_fusion
  330.1 8.7 %copy.97 = bf16[1,2,2048,128]{3,1,0,2:T(2,128)(2,1)S(1)} copy(bf16[1,2,2048,128]{3,2,1,0:T(8,128)(2,1)S(1)} %maximum_bitcast_fusion) | data formatting | bytes 2097152 | tf_op jit(solution)/shard_map/broadcast_in_dim | solution.py:117
  338.7 39.5 %all_to_all.66 = bf16[1,2,2048,128]{3,1,0,2:T(2,128)(2,1)S(1)} all-to-all(bf16[1,2,2048,128]{3,1,0,2:T(2,128)(2,1)S(1)} %copy.97), channel_id=1, replica_groups=mesh['branch'=2,'seq'=16,'mp'=8] {'seq'}, dimensions={2} | all-to-all | bytes 2097152 | tf_op jit(solution)/shard_map/all_to_all | solution.py:118
  378.4 0.7 copy.99
  379.1 1.3 copy.100
  (44 shorter events, 2.3 us)
Async XLA Ops:
  10.2 61.6 %all-to-all-start.2 = ((bf16[1,2,128,2048]{2,1,0,3:T(2,128)(2,1)}), bf16[1,2,128,2048]{2,1,0,3:T(2,128)(2,1)S(1)}, u32[]{:S(2)}, u32[]{:S(2)}) async-start(bf16[1,2,128,2048]{2,1,0,3:T(2,128)(2,1)} %copy.89), calls=%async_computation.2 | async-start | bytes 2097152 | tf_op jit(solution)/shard_map/all_to_all | solution.py:82
  20.2 24.7 %collective-permute-start = (bf16[1,2,128,2048]{3,2,1,0:T(8,128)(2,1)}, bf16[1,2,128,2048]{3,2,1,0:T(8,128)(2,1)S(1)}, u32[]{:S(2)}, u32[]{:S(2)}) collective-permute-start(bf16[1,2,128,2048]{3,2,1,0:T(8,128)(2,1)} %param.12), channel_id=1, source_target_pairs={{0,128},{128,0},{1,129},{129,1},{2,130},{130,2},{3,131},{131,3},{4... | collective-permute-start | bytes 3145736 | tf_op jit(solution)/shard_map/ppermute | solution.py:14
  21.5 45.9 %collective-permute-start.1 = (bf16[1,2,128,2048]{3,2,1,0:T(8,128)(2,1)}, bf16[1,2,128,2048]{3,2,1,0:T(8,128)(2,1)S(1)}, u32[]{:S(2)}, u32[]{:S(2)}) collective-permute-start(bf16[1,2,128,2048]{3,2,1,0:T(8,128)(2,1)} %param.13), channel_id=1, source_target_pairs={{0,128},{128,0},{1,129},{129,1},{2,130},{130,2},{3,131},{131,3},{4... | collective-permute-start | bytes 3145736 | tf_op jit(solution)/shard_map/ppermute | solution.py:14
  67.4 45.1 %copy-start.6 = (s32[2]{0:T(128)S(1)}, s32[2]{0:T(128)}, u32[]{:S(2)}) copy-start(s32[2]{0:T(128)} %param.16) | copy-start | bytes 28
  71.8 35.9 %all-to-all-start.1 = ((bf16[1,2,128,2048]{2,1,0,3:T(2,128)(2,1)}), bf16[1,2,128,2048]{2,1,0,3:T(2,128)(2,1)S(1)}, u32[]{:S(2)}, u32[]{:S(2)}) async-start(bf16[1,2,128,2048]{2,1,0,3:T(2,128)(2,1)} %copy.85), calls=%async_computation.1 | async-start | bytes 2097152 | tf_op jit(solution)/shard_map/all_to_all | solution.py:81
  107.7 1.0 copy-start
  108.7 31.4 %all-to-all-start = ((bf16[1,2,128,2048]{2,1,0,3:T(2,128)(2,1)}), bf16[1,2,128,2048]{2,1,0,3:T(2,128)(2,1)S(1)}, u32[]{:S(2)}, u32[]{:S(2)}) async-start(bf16[1,2,128,2048]{2,1,0,3:T(2,128)(2,1)} %copy.83), calls=%async_computation | async-start | bytes 2097152 | tf_op jit(solution)/shard_map/all_to_all | solution.py:80
  112.3 127.7 %all-reduce.5.cloned.1.call-start = ((), (), s32[]{:S(2)}) async-start(), calls=%async_computation.4 | async-start | bytes 4194304 | tf_op jit(solution)/shard_map/psum | solution.py:19
  118.3 7.0 %copy-start.5 = (s32[16,2]{0,1:T(2,128)S(1)}, s32[16,2]{0,1:T(2,128)}, u32[]{:S(2)}) copy-start(s32[16,2]{0,1:T(2,128)} %param.17) | copy-start | bytes 388
  239.9 4.6 %copy-start.1 = (bf16[1,1,16,128,128]{4,3,2,1,0:T(8,128)(2,1)S(1)}, bf16[1,1,16,128,128]{4,3,2,1,0:T(8,128)(2,1)}, u32[]{:S(2)}) copy-start(bf16[1,1,16,128,128]{4,3,2,1,0:T(8,128)(2,1)} %copy.87) | copy-start | bytes 1572868
  239.9 4.6 %copy-start.2 = (bf16[1,1,16,128,128]{4,3,2,1,0:T(8,128)(2,1)S(1)}, bf16[1,1,16,128,128]{4,3,2,1,0:T(8,128)(2,1)}, u32[]{:S(2)}) copy-start(bf16[1,1,16,128,128]{4,3,2,1,0:T(8,128)(2,1)} %copy.94) | copy-start | bytes 1572868
  248.6 3.3 copy-start.4
  259.3 3.3 copy-start.4
  269.9 3.3 copy-start.4
  280.6 3.3 copy-start.4
  291.5 3.3 copy-start.3
  301.6 3.3 copy-start.3
  311.7 3.3 copy-start.3
  321.8 3.3 copy-start.3
Sparse Core Ops, SparseCore 0:
  125.4 114.4 all-reduce.4
where the time goes:
time: 388 us; the launch traced here: 387 us
  waiting for transfers between devices  163 us (42%)
  matrix products  56.5 us (15%)
  other arithmetic  47.9 us (12%)
  blocking collectives  39.5 us (10%)
  local copies, waits for them, and re-layouts  38.3 us (10%)
  starting transfers between devices  23.1 us (6%)
  between operations  18.6 us (5%)
    psum x1, waiting for transfers between devices, from_root(): return lax.psum(block, axis)  97.8 us
    all_to_all x1, blocking collectives, local(): lax.all_to_all(attended, 'seq', split_axis=2, concat_axis=3, tiled=True)  39.5 us
    ppermute x2, waiting for transfers between devices, swapped(): return lax.ppermute(value, axis, pairs)  33.6 us
    dot_general x8, matrix products, one_block(): jnp.einsum('hqk,khd->qhd', rounded, value_whole, preferred_element_type=j...  32.3 us
    reduce_sum x8, other arithmetic, one_block(): totals = jnp.sum(weights, axis=2)  26.3 us
    all_to_all x1, waiting for transfers between devices, local(): lax.all_to_all(mixed_keys, 'seq', split_axis=3, concat_axis=2, tiled=True)  26 us
    dot_general x8, matrix products, score_tile(): jnp.einsum('qhd,khd->hqk', query_block, key_tile, preferred_element_type=...  24.2 us
    all_to_all x1, starting transfers between devices, local(): lax.all_to_all(values, 'seq', split_axis=3, concat_axis=2, tiled=True)  9.97 us
  transfers between devices with their start and end apart: 6, of which 5 were waited for; matrix products, arithmetic and copies ran while one was open for 10% of the time, Pallas kernels for 0%

commit v1 on v0

--- a/solution.py
+++ b/solution.py
@@ -16,7 +16,7 @@
 
 def from_root(block, axis, holder):
     block = jnp.where(lax.axis_index(axis) == holder, block, jnp.zeros_like(block))
-    return lax.psum(block, axis)
+    return jnp.sum(lax.all_gather(block, axis), axis=0)
 
 
 def blend_pair(source, partner, strength):

time: 388 us -> 515 us (1.33)
  waiting for transfers between devices: 163 us -> 261 us
  blocking collectives: 39.5 us -> 68.1 us
  other arithmetic: 47.9 us -> 61 us
  starting transfers between devices: 23.1 us -> 15.4 us
  local copies, waits for them, and re-layouts: 38.3 us -> 33.1 us
    all_gather x0 -> x4, waiting for transfers between devices: none -> 168 us  [from_root(): return jnp.sum(lax.all_gather(block, axis), axis=0)]
    psum x1 -> x0, waiting for transfers between devices: 97.8 us -> none  [from_root(): return lax.psum(block, axis)]
    all_to_all x0 -> x1, blocking collectives: none -> 31.5 us  [local(): lax.all_to_all(mixed_keys, 'seq', split_axis=3, concat_axis=2, tiled=True)]
    all_to_all x1 -> x0, waiting for transfers between devices: 26 us -> none  [local(): lax.all_to_all(mixed_keys, 'seq', split_axis=3, concat_axis=2, tiled=True)]
    all_to_all x1, waiting for transfers between devices: 0.01 us -> 21.6 us  [local(): lax.all_to_all(values, 'seq', split_axis=3, concat_axis=2, tiled=True)]
    ppermute x2, waiting for transfers between devices: 33.6 us -> 51 us  [swapped(): return lax.ppermute(value, axis, pairs)]
    all_to_all x1, waiting for transfers between devices: 5.48 us -> 19.4 us  [local(): lax.all_to_all(mixed_queries, 'seq', split_axis=3, concat_axis=2, tiled=T...]
    reduce_sum x0 -> x4, other arithmetic: none -> 12.2 us  [from_root(): return jnp.sum(lax.all_gather(block, axis), axis=0)]
  transfers between devices with their start and end apart: 6 -> 8, of which waited for: 5 -> 7; matrix products, arithmetic and copies ran while one was open for 10% -> 8% of each run, Pallas kernels for 0% -> 0%
where the time goes in v1:
time: 515 us; the launch traced here: 514 us
  waiting for transfers between devices  261 us (51%)
  blocking collectives  68.1 us (13%)
  other arithmetic  61 us (12%)
  matrix products  56.6 us (11%)
  local copies, waits for them, and re-layouts  33.1 us (6%)
  between operations  18.4 us (4%)
  starting transfers between devices  15.4 us (3%)
    all_gather x4, waiting for transfers between devices, from_root(): return jnp.sum(lax.all_gather(block, axis), axis=0)  168 us
    ppermute x2, waiting for transfers between devices, swapped(): return lax.ppermute(value, axis, pairs)  51 us
    all_to_all x1, blocking collectives, local(): lax.all_to_all(attended, 'seq', split_axis=2, concat_axis=3, tiled=True)  36.7 us
    dot_general x8, matrix products, one_block(): jnp.einsum('hqk,khd->qhd', rounded, value_whole, preferred_element_type=j...  32.4 us
    all_to_all x1, blocking collectives, local(): lax.all_to_all(mixed_keys, 'seq', split_axis=3, concat_axis=2, tiled=True)  31.5 us
    reduce_sum x8, other arithmetic, one_block(): totals = jnp.sum(weights, axis=2)  26.3 us
    dot_general x8, matrix products, score_tile(): jnp.einsum('qhd,khd->hqk', query_block, key_tile, preferred_element_type=...  24.2 us
    all_to_all x1, waiting for transfers between devices, local(): lax.all_to_all(values, 'seq', split_axis=3, concat_axis=2, tiled=True)  21.6 us
  transfers between devices with their start and end apart: 8, of which 7 were waited for; matrix products, arithmetic and copies ran while one was open for 8% of the time, Pallas kernels for 0%

profile of v1, /device:TPU:1, one launch (start us, length us, event | category | flops | bytes accessed | tf_op | source)
XLA Modules:
  0.0 513.9 jit_solution(15154636125270171756)
XLA Ops:
  6.5 3.8 copy.88
  10.3 10.0 %all-to-all-start.2 = ((bf16[1,2,128,2048]{2,1,0,3:T(2,128)(2,1)}), bf16[1,2,128,2048]{2,1,0,3:T(2,128)(2,1)S(1)}, u32[]{:S(2)}, u32[]{:S(2)}) async-start(bf16[1,2,128,2048]{2,1,0,3:T(2,128)(2,1)} %copy.88), calls=%async_computation.2 | async-start | bytes 2097152 | tf_op jit(solution)/shard_map/all_to_all | solution.py:82
  20.3 1.3 fusion.85
  26.7 21.6 %all-to-all-done.2 = bf16[1,2,128,2048]{2,1,0,3:T(2,128)(2,1)S(1)} async-done(((bf16[1,2,128,2048]{2,1,0,3:T(2,128)(2,1)}), bf16[1,2,128,2048]{2,1,0,3:T(2,128)(2,1)S(1)}, u32[]{:S(2)}, u32[]{:S(2)}) %all-to-all-start.2) | async-done | bytes 1048608 | tf_op jit(solution)/shard_map/all_to_all | solution.py:82
  49.1 1.1 dynamic-slice_select_fusion.1
  51.0 1.4 collective-permute-start
  53.3 4.3 compare_select_fusion.1
  57.8 5.7 %broadcast_subtract_fusion = (f32[2048]{0:T(1024)S(1)}, f32[2048]{0:T(1024)S(1)}) fusion(pred[2048]{0:T(1024)(128)(4,1)S(1)} %get-tuple-element.163, pred[2048]{0:T(1024)(128)(4,1)S(1)} %get-tuple-element.162, pred[2048]{0:T(1024)(128)(4,1)S(1)} %get-tuple-element.161, pred[2048]{0:T(1024)(128)(4,1)S(1)} %get-tuple-element.160, ...), kind=kLoop, calls=%fused_computation.76 | loop fusion | flops 38912 | bytes 43044 | tf_op jit(solution)/shard_map/sub | solution.py:24
  63.5 18.7 %collective-permute-done = bf16[1,2,128,2048]{3,2,1,0:T(8,128)(2,1)S(1)} collective-permute-done((bf16[1,2,128,2048]{3,2,1,0:T(8,128)(2,1)}, bf16[1,2,128,2048]{3,2,1,0:T(8,128)(2,1)S(1)}, u32[]{:S(2)}, u32[]{:S(2)}) %collective-permute-start) | collective-permute-done | bytes 1048608 | tf_op jit(solution)/shard_map/ppermute | solution.py:14
  82.2 32.4 %collective-permute-done.1 = bf16[1,2,128,2048]{3,2,1,0:T(8,128)(2,1)S(1)} collective-permute-done((bf16[1,2,128,2048]{3,2,1,0:T(8,128)(2,1)S(1)}, bf16[1,2,128,2048]{3,2,1,0:T(8,128)(2,1)S(1)}, u32[]{:S(2)}, u32[]{:S(2)}) %collective-permute-start.1) | collective-permute-done | bytes 1048608 | tf_op jit(solution)/shard_map/ppermute | solution.py:14
  114.5 3.4 add_convert_fusion
  117.9 0.8 copy.84
  118.7 31.5 %all_to_all.66 = bf16[1,2,128,2048]{2,1,0,3:T(2,128)(2,1)S(1)} all-to-all(bf16[1,2,128,2048]{2,1,0,3:T(2,128)(2,1)S(1)} %copy.84), channel_id=1, replica_groups=mesh['branch'=2,'seq'=16,'mp'=8] {'seq'}, dimensions={3} | all-to-all | bytes 2097152 | tf_op jit(solution)/shard_map/all_to_all | solution.py:81
  151.0 1.1 dynamic-slice_select_fusion.3
  152.7 3.7 copy.82
  156.4 3.7 all-to-all-start
  160.6 1.0 fusion.82
  161.6 2.1 copy.90
  163.7 2.0 copy.94
  165.8 1.0 copy.86
  166.8 1.0 copy.93
  167.9 19.4 %all-to-all-done = bf16[1,2,128,2048]{2,1,0,3:T(2,128)(2,1)S(1)} async-done(((bf16[1,2,128,2048]{2,1,0,3:T(2,128)(2,1)}), bf16[1,2,128,2048]{2,1,0,3:T(2,128)(2,1)S(1)}, u32[]{:S(2)}, u32[]{:S(2)}) %all-to-all-start) | async-done | bytes 1048608 | tf_op jit(solution)/shard_map/all_to_all | solution.py:80
  187.3 0.9 copy.83
  188.2 1.1 fusion.84
  189.3 3.1 reduce_sum.68
  192.3 20.4 %all-gather.11.cloned.1.call-done = bf16[8,2048,128]{2,1,0:T(8,128)(2,1)} async-done(((bf16[1,2048,128]{2,1,0:T(8,128)(2,1)}), bf16[8,2048,128]{2,1,0:T(8,128)(2,1)}) %all-gather.11.cloned.1.call-update) | async-done | bytes 4194320 | tf_op jit(solution)/shard_map/all_gather | solution.py:19
  212.7 3.1 reduce_sum.69
  215.8 1.1 pad_maximum_fusion.5
  216.9 73.2 %all-gather.5.cloned.1.call-done = bf16[8,2048,128]{2,1,0:T(8,128)(2,1)} async-done(((bf16[1,2048,128]{2,1,0:T(8,128)(2,1)}), bf16[8,2048,128]{2,1,0:T(8,128)(2,1)}) %all-gather.5.cloned.1.call-update) | async-done | bytes 4194320 | tf_op jit(solution)/shard_map/all_gather | solution.py:19
  290.0 3.1 reduce_sum.66
  293.1 74.1 %all-gather.7.cloned.1.call-done = bf16[8,2048,128]{2,1,0:T(8,128)(2,1)} async-done(((bf16[1,2048,128]{2,1,0:T(8,128)(2,1)}), bf16[8,2048,128]{2,1,0:T(8,128)(2,1)}) %all-gather.7.cloned.1.call-update) | async-done | bytes 4194320 | tf_op jit(solution)/shard_map/all_gather | solution.py:19
  367.1 3.1 reduce_sum.67
  370.3 4.2 pad_maximum_fusion.1
  374.5 0.9 broadcast.200.clone.1
  375.4 42.6 %while.21 = (s32[]{:T(128)}, bf16[4,512,128]{2,1,0:T(8,128)(2,1)}, pred[6144]{0:T(1024)(128)(4,1)S(1)}, bf16[4,512,1,128]{3,1,2,0:T(8,128)(2,1)}, bf16[6144,1,12...) while((s32[]{:T(128)}, bf16[4,512,128]{2,1,0:T(8,128)(2,1)}, ...), condition=%wide.region_7.8_spmd, body=%wide.region_4.7_spmd.sunk | while | flops 1651637248 | bytes 47477864 | solution.py:69
  375.4 3.0 fusion.99
  378.4 3.3 fusion.100
  381.7 4.3 fusion.101
  386.0 3.0 fusion.99
  389.1 3.3 fusion.100
  392.4 4.3 fusion.101
  396.7 3.0 fusion.99
  399.7 3.3 fusion.100
  403.0 4.3 fusion.101
  407.4 3.0 fusion.99
  410.4 3.3 fusion.100
  413.7 4.3 fusion.101
  418.1 40.7 %while.22 = (s32[]{:T(128)}, bf16[4,512,128]{2,1,0:T(8,128)(2,1)S(1)}, pred[6144]{0:T(1024)(128)(4,1)S(1)}, bf16[4,512,1,128]{3,1,2,0:T(8,128)(2,1)}, bf16[6144,...) while((s32[]{:T(128)}, bf16[4,512,128]{2,1,0:T(8,128)(2,1)S(1)}, ...), condition=%wide.region_11.12_spmd, body=%wide.region_8.11_spmd.sunk | while | flops 1651637248 | bytes 47477356 | solution.py:69
  418.3 3.0 fusion.104
  421.4 3.3 fusion.105
  424.7 3.8 fusion.106
  428.4 3.0 fusion.104
  431.5 3.3 fusion.105
  434.8 3.8 fusion.106
  438.5 3.0 fusion.104
  441.6 3.3 fusion.105
  444.9 3.8 fusion.106
  448.6 3.0 fusion.104
  451.7 3.3 fusion.105
  455.0 3.8 fusion.106
  458.8 1.1 maximum_bitcast_fusion
  459.9 8.7 %copy.96 = bf16[1,2,2048,128]{3,1,0,2:T(2,128)(2,1)S(1)} copy(bf16[1,2,2048,128]{3,2,1,0:T(8,128)(2,1)S(1)} %maximum_bitcast_fusion) | data formatting | bytes 2097152 | tf_op jit(solution)/shard_map/broadcast_in_dim | solution.py:117
  468.6 36.7 %all_to_all.67 = bf16[1,2,2048,128]{3,1,0,2:T(2,128)(2,1)S(1)} all-to-all(bf16[1,2,2048,128]{3,1,0,2:T(2,128)(2,1)S(1)} %copy.96), channel_id=1, replica_groups=mesh['branch'=2,'seq'=16,'mp'=8] {'seq'}, dimensions={2} | all-to-all | bytes 2097152 | tf_op jit(solution)/shard_map/all_to_all | solution.py:118
  506.1 1.3 copy.99
  (52 shorter events, 5.7 us)
Async XLA Ops:
  6.5 45.8 %copy-start.2 = (bf16[1,2,128,2048]{3,2,1,0:T(8,128)(2,1)S(1)}, bf16[1,2,128,2048]{3,2,1,0:T(8,128)(2,1)}, u32[]{:S(2)}) copy-start(bf16[1,2,128,2048]{3,2,1,0:T(8,128)(2,1)} %param.13) | copy-start | bytes 3145732
  6.5 46.0 %copy-start.3 = (f32[1,16]{1,0:T(1,128)S(1)}, f32[1,16]{1,0:T(1,128)}, u32[]{:S(2)}) copy-start(f32[1,16]{1,0:T(1,128)} %param.15) | copy-start | bytes 196
  10.3 38.0 %all-to-all-start.2 = ((bf16[1,2,128,2048]{2,1,0,3:T(2,128)(2,1)}), bf16[1,2,128,2048]{2,1,0,3:T(2,128)(2,1)S(1)}, u32[]{:S(2)}, u32[]{:S(2)}) async-start(bf16[1,2,128,2048]{2,1,0,3:T(2,128)(2,1)} %copy.88), calls=%async_computation.2 | async-start | bytes 2097152 | tf_op jit(solution)/shard_map/all_to_all | solution.py:82
  20.3 169.0 %all-gather.9.cloned.1.call-start = ((), (), s32[]{:S(2)}) async-start(), calls=%async_computation.6 | async-start | bytes 4718592 | tf_op jit(solution)/shard_map/all_gather | solution.py:19
  50.2 162.5 %all-gather.11.cloned.1.call-start = ((), (), s32[]{:S(2)}) async-start(), calls=%async_computation.7 | async-start | bytes 4718592 | tf_op jit(solution)/shard_map/all_gather | solution.py:19
  50.9 239.1 %all-gather.5.cloned.1.call-start = ((), (), s32[]{:S(2)}) async-start(), calls=%async_computation.4 | async-start | bytes 4718592 | tf_op jit(solution)/shard_map/all_gather | solution.py:19
  51.0 31.2 %collective-permute-start = (bf16[1,2,128,2048]{3,2,1,0:T(8,128)(2,1)}, bf16[1,2,128,2048]{3,2,1,0:T(8,128)(2,1)S(1)}, u32[]{:S(2)}, u32[]{:S(2)}) collective-permute-start(bf16[1,2,128,2048]{3,2,1,0:T(8,128)(2,1)} %param.12), channel_id=1, source_target_pairs={{0,128},{128,0},{1,129},{129,1},{2,130},{130,2},{3,131},{131,3},{4... | collective-permute-start | bytes 3145736 | tf_op jit(solution)/shard_map/ppermute | solution.py:14
  52.4 62.2 %collective-permute-start.1 = (bf16[1,2,128,2048]{3,2,1,0:T(8,128)(2,1)S(1)}, bf16[1,2,128,2048]{3,2,1,0:T(8,128)(2,1)S(1)}, u32[]{:S(2)}, u32[]{:S(2)}) collective-permute-start(bf16[1,2,128,2048]{3,2,1,0:T(8,128)(2,1)S(1)} %copy-done.2), channel_id=1, source_target_pairs={{0,128},{128,0},{1,129},{129,1},{2,130},{130,2},{3,131},{131,3},{4... | collective-permute-start | bytes 3145736 | tf_op jit(solution)/shard_map/ppermute | solution.py:14
  150.2 9.9 %copy-start.4 = (s32[16,2]{0,1:T(2,128)S(1)}, s32[16,2]{0,1:T(2,128)}, u32[]{:S(2)}) copy-start(s32[16,2]{0,1:T(2,128)} %param.17) | copy-start | bytes 388
  152.1 215.0 %all-gather.7.cloned.1.call-start = ((), (), s32[]{:S(2)}) async-start(), calls=%async_computation.5 | async-start | bytes 4718592 | tf_op jit(solution)/shard_map/all_gather | solution.py:19
  156.4 30.9 %all-to-all-start = ((bf16[1,2,128,2048]{2,1,0,3:T(2,128)(2,1)}), bf16[1,2,128,2048]{2,1,0,3:T(2,128)(2,1)S(1)}, u32[]{:S(2)}, u32[]{:S(2)}) async-start(bf16[1,2,128,2048]{2,1,0,3:T(2,128)(2,1)} %copy.82), calls=%async_computation | async-start | bytes 2097152 | tf_op jit(solution)/shard_map/all_to_all | solution.py:80
  378.4 3.3 copy-start.1
  389.1 3.3 copy-start.1
  399.7 3.3 copy-start.1
  410.4 3.3 copy-start.1
  421.4 3.3 copy-start
  431.5 3.3 copy-start
  441.6 3.3 copy-start
  451.7 3.3 copy-start
Sparse Core Ops, SparseCore 0:
  50.3 88.9 all-gather.8
  142.0 70.7 all-gather.10
  215.4 74.6 all-gather.4
  292.5 74.6 all-gather.6
